TPU v7x, 256 devices: a whole 4x4x8 slice. The times are simulated.
256 devices in a mesh: dp: 16 (over z, core), ctx: 4 (over x), head: 4 (over y).
Axes of the slice: x: 4, y: 4, z: 8, core: 2. Of those that a mesh axis runs over, the one named last changes fastest.
Arguments:
- hidden_in: bfloat16 [16, 2048, 8192], P('dp', 'ctx', 'head'), may hold values from -40 to 40
- w_query: bfloat16 [8192, 4096], P('dp', 'head'), may hold values from -0.0625 to 0.0625
- w_key: bfloat16 [8192, 512], P('dp', 'head'), may hold values from -0.0625 to 0.0625
- w_value: bfloat16 [8192, 512], P('dp', 'head'), may hold values from -0.0625 to 0.0625
- mem_gate: float32 [32], P('head'), may hold values from -3 to 3
Outputs:
- attended: bfloat16 [16, 2048, 4096], P('dp', 'ctx', 'head')
All inputs are finite; a program needn't handle non-finite values.
Results may differ from a plain program's by a relative error of at most 0.011.
Values may be sent and summed in bfloat16 or wider, within the bound.
A program may use at most 128 MiB of HBM per device.

v0:
```python
import math
import jax
import jax.numpy as jnp
from jax import lax
from jax.sharding import PartitionSpec as P

HD = 128
SEG = 128


def entering(shard, axis, combine, identity):
    peers, index = (lax.axis_size(axis), lax.axis_index(axis))
    everything = jax.tree.map(
        lambda part, kind: lax.all_gather(part.astype(kind), axis),
        shard,
        (jnp.bfloat16, jnp.bfloat16),
    )
    start = jax.tree.map(
        lambda part, zero: jnp.broadcast_to(jnp.asarray(zero, part.dtype), part.shape),
        shard,
        identity,
    )

    def lap(k, before):
        reached = k < index
        new = combine(
            before, jax.tree.map(lambda part, own: part[k].astype(own.dtype), everything, shard)
        )
        return jax.tree.map(lambda a, b: jnp.where(reached, a, b), new, before)

    return lax.fori_loop(0, peers, lap, start)


def feature_map(vector):
    return jax.nn.elu(vector) + 1.0


def exclusive_sum(stack):
    running = jnp.cumsum(stack, axis=0)
    return jnp.concatenate([jnp.zeros_like(stack[:1]), running[:-1]], axis=0)


def add_pair(earlier, later):
    return (earlier[0] + later[0], earlier[1] + later[1])


def body(hidden_in, w_query, w_key, w_value, mem_gate):
    highest = lax.Precision.HIGHEST
    features = lax.all_gather(hidden_in, "head", axis=2, tiled=True)
    tok_rows = features.shape[1]
    flattened = features[0]
    query_full = jnp.dot(
        flattened,
        lax.all_gather(w_query, "dp", axis=0, tiled=True),
        preferred_element_type=jnp.float32,
    )
    keys_full = jnp.dot(
        flattened,
        lax.all_gather(w_key, "dp", axis=0, tiled=True),
        preferred_element_type=jnp.float32,
    )
    values_full = jnp.dot(
        flattened,
        lax.all_gather(w_value, "dp", axis=0, tiled=True),
        preferred_element_type=jnp.float32,
    )
    query = query_full.astype(jnp.bfloat16)
    keys = keys_full.astype(jnp.bfloat16)
    values = values_full.astype(jnp.bfloat16)
    heads_dev = query.shape[1] // HD
    kv_dev = keys.shape[1] // HD
    group_size = heads_dev // kv_dev
    segments = tok_rows // SEG
    query_seg = query.reshape(segments, SEG, kv_dev, group_size, HD)
    key_seg = keys.reshape(segments, SEG, kv_dev, HD)
    value_seg = values.reshape(segments, SEG, kv_dev, HD)
    scores = jnp.einsum(
        "nqkgd,nskd->nkgqs", query_seg, key_seg, preferred_element_type=jnp.float32
    ) / math.sqrt(HD)
    causal = jnp.arange(SEG)[:, None] >= jnp.arange(SEG)[None, :]
    scores = jnp.where(causal, scores, -jnp.inf)
    probs = jax.nn.softmax(scores, axis=-1).astype(jnp.bfloat16)
    local = jnp.einsum("nkgqs,nskd->nqkgd", probs, value_seg, preferred_element_type=jnp.float32)
    value_wide = value_seg.astype(jnp.float32)
    feat_key = feature_map(key_seg.astype(jnp.float32))
    increment = jnp.einsum("nskd,nske->nkde", feat_key, value_wide, precision=highest)
    key_mass = jnp.sum(feat_key, axis=1)
    state_total = jnp.sum(increment, axis=0)
    mass_total = jnp.sum(key_mass, axis=0)
    prior_state, prior_mass = entering(
        (state_total, mass_total),
        "ctx",
        add_pair,
        (jnp.zeros_like(state_total), jnp.zeros_like(mass_total)),
    )
    memory = prior_state[None] + exclusive_sum(increment)
    mass_prior = prior_mass[None] + exclusive_sum(key_mass)
    feat_query = feature_map(query_seg.astype(jnp.float32))
    numerator = jnp.einsum("nqkgd,nkde->nqkge", feat_query, memory, precision=highest)
    denominator = jnp.einsum("nqkgd,nkd->nqkg", feat_query, mass_prior, precision=highest) + 1.0
    retrieved = numerator / denominator[..., None]
    gate_share = jax.nn.sigmoid(mem_gate).reshape(kv_dev, group_size)[None, None, :, :, None]
    mixed = gate_share * retrieved + (1.0 - gate_share) * local
    return mixed.reshape(1, tok_rows, heads_dev * HD).astype(jnp.bfloat16)


def solution(mesh):
    return jax.shard_map(
        body,
        mesh=mesh,
        in_specs=(
            P("dp", "ctx", "head"),
            P("dp", "head"),
            P("dp", "head"),
            P("dp", "head"),
            P("head"),
        ),
        out_specs=P("dp", "ctx", "head"),
        check_vma=False,
    )
```

profile of v0, /device:TPU:1, one launch (start us, length us, event | category | flops | bytes accessed | tf_op | source)
XLA Modules:
  0.0 307.1 jit_solution(8610718658696810357)
XLA Ops:
  6.5 0.0 copy-start.1
  6.5 0.0 all-gather.12.cloned.1.call-start
  6.5 0.7 all-gather.12.cloned.1.call-update
  7.3 0.0 all-gather.8.cloned.1.call-start
  7.3 0.7 all-gather.8.cloned.1.call-update
  8.0 0.0 all-gather.10.cloned.1.call-start
  8.1 0.7 all-gather.10.cloned.1.call-update
  8.7 0.0 all-gather.14.cloned.1.call-start
  8.8 0.5 all-gather.14.cloned.1.call-update
  9.4 0.0 copy-done.1
  9.4 43.4 %all-gather.12.cloned.1.call-done = bf16[8192,128]{1,0:T(8,128)(2,1)} async-done(((bf16[512,128]{1,0:T(8,128)(2,1)}), bf16[8192,128]{1,0:T(8,128)(2,1)}) %all-gather.12.cloned.1.call-update) | async-done | bytes 2097168 | tf_op jit(solution)/shard_map/all_gather | solution.py:64
  52.8 85.3 %all-gather.8.cloned.1.call-done = bf16[1,512,8192]{2,1,0:T(8,128)(2,1)} async-done(((bf16[1,512,2048]{2,1,0:T(8,128)(2,1)}), bf16[1,512,8192]{2,1,0:T(8,128)(2,1)}) %all-gather.8.cloned.1.call-update) | async-done | bytes 8388624 | tf_op jit(solution)/shard_map/all_gather | solution.py:49
  138.1 6.3 %fusion.24 = bf16[512,128]{1,0:T(8,128)(2,1)S(1)} fusion(bf16[8192,128]{1,0:T(8,128)(2,1)} %all-gather.12.cloned.1.call-done, bf16[1,512,8192]{2,1,0:T(8,128)(2,1)} %all-gather.8.cloned.1.call-done), kind=kOutput, calls=%fused_computation.27 | convolution fusion | flops 1073807360 | bytes 10616832 | tf_op jit(solution)/shard_map/dot_general | solution.py:62
  144.4 36.5 %all-gather.10.cloned.1.call-done = bf16[8192,128]{1,0:T(8,128)(2,1)} async-done(((bf16[512,128]{1,0:T(8,128)(2,1)}), bf16[8192,128]{1,0:T(8,128)(2,1)}) %all-gather.10.cloned.1.call-update) | async-done | bytes 2097168 | tf_op jit(solution)/shard_map/all_gather | solution.py:59
  180.9 6.3 %fusion.42 = (bf16[128]{0:T(256)(128)(2,1)S(1)}, bf16[512,128]{1,0:T(8,128)(2,1)S(1)}) fusion(bf16[8192,128]{1,0:T(8,128)(2,1)} %all-gather.10.cloned.1.call-done, bf16[1,512,8192]{2,1,0:T(8,128)(2,1)} %all-gather.8.cloned.1.call-done), kind=kOutput, calls=%fused_computation.48 | convolution fusion | flops 1074200448 | bytes 10617088 | tf_op jit(solution)/shard_map/dot_general | solution.py:57
  187.3 0.5 fusion.64
  187.7 0.2 fusion.47
  187.9 0.0 copy-start
  187.9 0.1 fusion.45
  188.1 7.6 %all-gather.2 = bf16[4,1,128]{2,1,0:T(2,128)(2,1)S(1)} all-gather(bf16[1,1,128]{2,1,0:T(2,128)(2,1)S(1)} %bitcast.115), channel_id=3, replica_groups=mesh['dp'=16,'ctx'=4,'head'=4] {'ctx'}, dimensions={0}, use_global_device_ids=true | all-gather | bytes 1280 | tf_op jit(solution)/shard_map/all_gather | solution.py:14
  195.7 10.5 %all-gather = bf16[512,128]{1,0:T(8,128)(2,1)S(1)} all-gather(bf16[128,128]{1,0:T(8,128)(2,1)S(1)} %get-tuple-element.152), channel_id=2, replica_groups=mesh['dp'=16,'ctx'=4,'head'=4] {'ctx'}, dimensions={0}, use_global_device_ids=true | all-gather | bytes 163840 | tf_op jit(solution)/shard_map/all_gather | solution.py:14
  206.2 0.2 while.16
  206.4 70.0 %all-gather.14.cloned.1.call-done = bf16[8192,1024]{1,0:T(8,128)(2,1)} async-done(((bf16[512,1024]{1,0:T(8,128)(2,1)}), bf16[8192,1024]{1,0:T(8,128)(2,1)}) %all-gather.14.cloned.1.call-update) | async-done | bytes 16777232 | tf_op jit(solution)/shard_map/all_gather | solution.py:54
  276.4 14.8 %fusion.18 = bf16[64,8,8,128]{3,1,2,0:T(8,128)(2,1)S(1)} fusion(bf16[8192,1024]{1,0:T(8,128)(2,1)} %all-gather.14.cloned.1.call-done, bf16[1,512,8192]{2,1,0:T(8,128)(2,1)} %all-gather.8.cloned.1.call-done), kind=kOutput, calls=%fused_computation.25 | convolution fusion | flops 8590458880 | bytes 26214400 | tf_op jit(solution)/shard_map/dot_general | solution.py:52
  291.2 0.0 copy-done
  291.2 0.3 copy.37
  291.5 0.0 slice-start
  291.5 2.5 fusion.10
  294.1 0.0 slice-done
  294.1 2.8 fusion.12
  296.9 0.5 fusion.65
  297.3 0.4 fusion.14
  297.7 0.8 fusion.8
  298.5 0.7 copy.25
  299.3 1.3 convert_element_type.134
  (15 shorter events, 0.2 us)
Async XLA Ops:
  6.5 2.8 copy-start.1
  6.5 46.3 %all-gather.12.cloned.1.call-start = ((), (), s32[]{:S(2)}) async-start(), calls=%async_computation.2 | async-start | bytes 2228224 | tf_op jit(solution)/shard_map/all_gather | solution.py:64
  7.3 130.9 %all-gather.8.cloned.1.call-start = ((), (), s32[]{:S(2)}) async-start(), calls=%async_computation | async-start | bytes 10485760 | tf_op jit(solution)/shard_map/all_gather | solution.py:49
  8.0 172.9 %all-gather.10.cloned.1.call-start = ((), (), s32[]{:S(2)}) async-start(), calls=%async_computation.1 | async-start | bytes 2228224 | tf_op jit(solution)/shard_map/all_gather | solution.py:59
  8.7 267.7 %all-gather.14.cloned.1.call-start = ((), (), s32[]{:S(2)}) async-start(), calls=%async_computation.3 | async-start | bytes 17825792 | tf_op jit(solution)/shard_map/all_gather | solution.py:54
  187.9 103.3 %copy-start = (f32[4,1,128,128]{3,2,0,1:T(8,128)}, f32[4,1,128,128]{3,2,0,1:T(8,128)S(1)}, u32[]{:S(2)}) copy-start(f32[4,1,128,128]{3,2,0,1:T(8,128)S(1)} %fusion.47) | copy-start | bytes 786436
  291.5 2.5 slice-start
Sparse Core Ops, SparseCore 0:
  9.2 43.6 all-gather.11
  54.6 83.4 all-gather.7
  139.9 40.9 all-gather.9
  182.6 93.7 all-gather.13
where the time goes:
time: 307 us
  waiting for transfers between devices  238 us (78%)
  matrix products  34.5 us (11%)
  blocking collectives  18.1 us (6%)
  between operations  13.3 us (4%)
    all_gather x1, waiting for transfers between devices, body(): features = lax.all_gather(hidden_in, 'head', axis=2, tiled=True)  85.3 us
    all_gather x1, waiting for transfers between devices, body(): lax.all_gather(w_query, 'dp', axis=0, tiled=True)  70 us
    all_gather x1, waiting for transfers between devices, body(): lax.all_gather(w_value, 'dp', axis=0, tiled=True)  43.4 us
    all_gather x1, waiting for transfers between devices, body(): lax.all_gather(w_key, 'dp', axis=0, tiled=True)  36.5 us
    all_gather x2, blocking collectives, entering(): lax.all_gather(part.astype(kind), axis)  18.1 us
    dot_general x1, matrix products, body(): jnp.dot(flattened, lax.all_gather(w_query, 'dp', axis=0, tiled=True), pre...  14.8 us
    dot_general x1, matrix products, body(): jnp.dot(flattened, lax.all_gather(w_key, 'dp', axis=0, tiled=True), prefe...  6.33 us
    dot_general x1, matrix products, body(): jnp.dot(flattened, lax.all_gather(w_value, 'dp', axis=0, tiled=True), pre...  6.3 us
  transfers between devices with their start and end apart: 4, of which 4 were waited for; matrix products, arithmetic and copies ran while one was open for 4% of the time, Pallas kernels for 0%

commit v1 on v0

--- a/solution.py
+++ b/solution.py
@@ -6,6 +6,28 @@
 
 HD = 128
 SEG = 128
+
+
+def joined_along(blocks, dim):
+    dims = list(blocks.shape[1:])
+    dims[dim] *= blocks.shape[0]
+    return jnp.moveaxis(blocks, 0, dim).reshape(dims)
+
+
+def collected_by_bits(x, axis):
+    peers = lax.axis_size(axis)
+    pieces = x[None]
+    for level in range(peers.bit_length() - 1):
+        stride = 1 << level
+        other = lax.ppermute(pieces, axis, [(i, i ^ stride) for i in range(peers)])
+        both = jnp.stack([pieces, other])
+        upper = lax.axis_index(axis) >> level & 1
+        pieces = jnp.where(upper == 0, both, both[::-1]).reshape(-1, *x.shape)
+    return pieces
+
+
+def gather_by_bits(x, axis, dim):
+    return joined_along(collected_by_bits(x, axis), dim)
 
 
 def entering(shard, axis, combine, identity):
@@ -60,9 +82,7 @@
         preferred_element_type=jnp.float32,
     )
     values_full = jnp.dot(
-        flattened,
-        lax.all_gather(w_value, "dp", axis=0, tiled=True),
-        preferred_element_type=jnp.float32,
+        flattened, gather_by_bits(w_value, "dp", 0), preferred_element_type=jnp.float32
     )
     query = query_full.astype(jnp.bfloat16)
     keys = keys_full.astype(jnp.bfloat16)

time: 307 us -> 268 us (0.87)
  waiting for transfers between devices: 238 us -> 187 us
  starting transfers between devices: 0.12 us -> 10.3 us
    all_gather x1, waiting for transfers between devices: 85.3 us -> 0.02 us  [body(): features = lax.all_gather(hidden_in, 'head', axis=2, tiled=True)]
    ppermute x0 -> x4, waiting for transfers between devices: none -> 78.1 us  [collected_by_bits(): other = lax.ppermute(pieces, axis, [(i, i ^ stride) for i in range(peers)])]
    all_gather x1 -> x0, waiting for transfers between devices: 43.4 us -> none  [body(): lax.all_gather(w_value, 'dp', axis=0, tiled=True)]
    ppermute x0 -> x4, starting transfers between devices: none -> 10.2 us  [collected_by_bits(): other = lax.ppermute(pieces, axis, [(i, i ^ stride) for i in range(peers)])]
  transfers between devices with their start and end apart: 4 -> 7, of which waited for: 4 -> 6; matrix products, arithmetic and copies ran while one was open for 4% -> 6% of each run, Pallas kernels for 0% -> 0%
where the time goes in v1:
time: 268 us
  waiting for transfers between devices  187 us (70%)
  matrix products  34.4 us (13%)
  blocking collectives  18.1 us (7%)
  between operations  13.3 us (5%)
  starting transfers between devices  10.3 us (4%)
    ppermute x4, waiting for transfers between devices, collected_by_bits(): other = lax.ppermute(pieces, axis, [(i, i ^ stride) for i in range(peers)])  78.1 us
    all_gather x1, waiting for transfers between devices, body(): lax.all_gather(w_query, 'dp', axis=0, tiled=True)  70.1 us
    all_gather x1, waiting for transfers between devices, body(): lax.all_gather(w_key, 'dp', axis=0, tiled=True)  36.5 us
    all_gather x2, blocking collectives, entering(): lax.all_gather(part.astype(kind), axis)  18.1 us
    dot_general x1, matrix products, body(): jnp.dot(flattened, lax.all_gather(w_query, 'dp', axis=0, tiled=True), pre...  14.8 us
    ppermute x4, starting transfers between devices, collected_by_bits(): other = lax.ppermute(pieces, axis, [(i, i ^ stride) for i in range(peers)])  10.2 us
    dot_general x1, matrix products, body(): jnp.dot(flattened, lax.all_gather(w_key, 'dp', axis=0, tiled=True), prefe...  6.33 us
    dot_general x1, matrix products, body(): jnp.dot(flattened, gather_by_bits(w_value, 'dp', 0), preferred_element_ty...  6.28 us
  transfers between devices with their start and end apart: 7, of which 6 were waited for; matrix products, arithmetic and copies ran while one was open for 6% of the time, Pallas kernels for 0%

profile of v1, /device:TPU:1, one launch (start us, length us, event | category | flops | bytes accessed | tf_op | source)
XLA Modules:
  0.0 267.5 jit_solution(13899732575108269139)
XLA Ops:
  6.5 0.0 copy-start.1
  6.5 0.0 all-gather.7.cloned.1.call-start
  6.5 0.7 all-gather.7.cloned.1.call-update
  7.3 0.0 all-gather.9.cloned.1.call-start
  7.3 0.7 all-gather.9.cloned.1.call-update
  8.0 0.0 all-gather.11.cloned.1.call-start
  8.1 0.7 all-gather.11.cloned.1.call-update
  8.7 0.0 copy-done.1
  8.8 3.3 %collective-permute-start = (bf16[1,512,128]{2,1,0:T(8,128)(2,1)S(1)}, bf16[1,512,128]{2,1,0:T(8,128)(2,1)S(1)}, u32[]{:S(2)}, u32[]{:S(2)}) collective-permute-start(bf16[1,512,128]{2,1,0:T(8,128)(2,1)S(1)} %bitcast.143), channel_id=1, source_target_pairs={{0,16},{16,0},{32,48},{48,32},{64,80},{80,64},{96,112},{112,96},{1... | collective-permute-start | bytes 393224 | tf_op jit(solution)/shard_map/ppermute | solution.py:22
  12.0 1.0 collective-permute-done
  13.1 0.1 fusion.52
  13.1 0.1 collective-permute-start.1
  13.2 7.5 %collective-permute-done.1 = bf16[2,512,128]{2,1,0:T(8,128)(2,1)S(1)} collective-permute-done((bf16[2,512,128]{2,1,0:T(8,128)(2,1)S(1)}, bf16[2,512,128]{2,1,0:T(8,128)(2,1)S(1)}, u32[]{:S(2)}, u32[]{:S(2)}) %collective-permute-start.1) | collective-permute-done | bytes 262176 | tf_op jit(solution)/shard_map/ppermute | solution.py:22
  20.7 0.1 pad_maximum_fusion.2
  20.8 0.1 reverse_select_fusion.2
  20.9 1.7 collective-permute-start.2
  22.6 24.2 %collective-permute-done.2 = bf16[4,512,128]{2,1,0:T(8,128)(2,1)S(1)} collective-permute-done((bf16[4,512,128]{2,1,0:T(8,128)(2,1)S(1)}, bf16[4,512,128]{2,1,0:T(8,128)(2,1)S(1)}, u32[]{:S(2)}, u32[]{:S(2)}) %collective-permute-start.2) | collective-permute-done | bytes 524320 | tf_op jit(solution)/shard_map/ppermute | solution.py:22
  46.8 0.1 pad_maximum_fusion.1
  46.9 0.2 reverse_select_fusion.1
  47.1 5.1 %collective-permute-start.3 = (bf16[8,512,128]{2,1,0:T(8,128)(2,1)S(1)}, bf16[8,512,128]{2,1,0:T(8,128)(2,1)S(1)}, u32[]{:S(2)}, u32[]{:S(2)}) collective-permute-start(bf16[8,512,128]{2,1,0:T(8,128)(2,1)S(1)} %bitcast.129), channel_id=1, source_target_pairs={{0,128},{16,144},{32,160},{48,176},{64,192},{80,208},{96,224},{112... | collective-permute-start | bytes 3145736 | tf_op jit(solution)/shard_map/ppermute | solution.py:22
  52.2 0.0 copy-done.2
  52.3 45.5 %collective-permute-done.3 = bf16[8,512,128]{2,1,0:T(8,128)(2,1)S(1)} collective-permute-done((bf16[8,512,128]{2,1,0:T(8,128)(2,1)S(1)}, bf16[8,512,128]{2,1,0:T(8,128)(2,1)S(1)}, u32[]{:S(2)}, u32[]{:S(2)}) %collective-permute-start.3) | collective-permute-done | bytes 1048608 | tf_op jit(solution)/shard_map/ppermute | solution.py:22
  97.7 0.2 pad_maximum_fusion
  97.9 0.5 reverse_select_fusion
  98.5 0.0 all-gather.7.cloned.1.call-done
  98.5 6.3 %fusion.24 = bf16[128,512]{1,0:T(8,128)(2,1)S(1)} fusion(bf16[8192,128]{1,0:T(8,128)(2,1)S(1)} %bitcast.125, bf16[1,512,8192]{2,1,0:T(8,128)(2,1)} %all-gather.7.cloned.1.call-done), kind=kOutput, calls=%fused_computation.30 | convolution fusion | flops 1073807360 | bytes 10616832 | tf_op jit(solution)/shard_map/dot_general | solution.py:84
  104.8 36.5 %all-gather.9.cloned.1.call-done = bf16[8192,128]{1,0:T(8,128)(2,1)} async-done(((bf16[512,128]{1,0:T(8,128)(2,1)}), bf16[8192,128]{1,0:T(8,128)(2,1)}) %all-gather.9.cloned.1.call-update) | async-done | bytes 2097168 | tf_op jit(solution)/shard_map/all_gather | solution.py:81
  141.3 6.3 %fusion.42 = (bf16[128]{0:T(256)(128)(2,1)S(1)}, bf16[512,128]{1,0:T(8,128)(2,1)S(1)}) fusion(bf16[8192,128]{1,0:T(8,128)(2,1)} %all-gather.9.cloned.1.call-done, bf16[1,512,8192]{2,1,0:T(8,128)(2,1)} %all-gather.7.cloned.1.call-done), kind=kOutput, calls=%fused_computation.55 | convolution fusion | flops 1074200448 | bytes 10617088 | tf_op jit(solution)/shard_map/dot_general | solution.py:79
  147.6 0.5 fusion.69
  148.1 0.2 fusion.47
  148.2 0.0 copy-start
  148.2 0.1 fusion.45
  148.4 7.6 %all-gather.2 = bf16[4,1,128]{2,1,0:T(2,128)(2,1)S(1)} all-gather(bf16[1,1,128]{2,1,0:T(2,128)(2,1)S(1)} %bitcast.149), channel_id=3, replica_groups=mesh['dp'=16,'ctx'=4,'head'=4] {'ctx'}, dimensions={0}, use_global_device_ids=true | all-gather | bytes 1280 | tf_op jit(solution)/shard_map/all_gather | solution.py:36
  156.1 10.5 %all-gather = bf16[512,128]{1,0:T(8,128)(2,1)S(1)} all-gather(bf16[128,128]{1,0:T(8,128)(2,1)S(1)} %get-tuple-element.154), channel_id=2, replica_groups=mesh['dp'=16,'ctx'=4,'head'=4] {'ctx'}, dimensions={0}, use_global_device_ids=true | all-gather | bytes 163840 | tf_op jit(solution)/shard_map/all_gather | solution.py:36
  166.6 0.2 while.16
  166.8 70.1 %all-gather.11.cloned.1.call-done = bf16[8192,1024]{1,0:T(8,128)(2,1)} async-done(((bf16[512,1024]{1,0:T(8,128)(2,1)}), bf16[8192,1024]{1,0:T(8,128)(2,1)}) %all-gather.11.cloned.1.call-update) | async-done | bytes 16777232 | tf_op jit(solution)/shard_map/all_gather | solution.py:76
  236.9 14.8 %fusion.18 = bf16[64,8,8,128]{3,1,2,0:T(8,128)(2,1)S(1)} fusion(bf16[8192,1024]{1,0:T(8,128)(2,1)} %all-gather.11.cloned.1.call-done, bf16[1,512,8192]{2,1,0:T(8,128)(2,1)} %all-gather.7.cloned.1.call-done), kind=kOutput, calls=%fused_computation.28 | convolution fusion | flops 8590458880 | bytes 26214400 | tf_op jit(solution)/shard_map/dot_general | solution.py:74
  251.7 0.0 copy-done
  251.7 0.3 copy.41
  251.9 0.0 slice-start
  252.0 2.5 fusion.10
  254.5 0.0 slice-done
  254.5 2.8 %fusion.12 = f32[4,128,128,8]{2,1,3,0:T(8,128)S(1)} fusion(bf16[4,128,8,128]{3,2,1,0:T(8,128)(2,1)S(1)} %bitcast.127, f32[3,1,128,128]{3,2,0,1:T(8,128)S(1)} %slice-done, f32[128,128]{1,0:T(8,128)S(1)} %bitcast.133), kind=kOutput, calls=%fused_computation.24 | convolution fusion | flops 807993344 | bytes 3407872 | tf_op jit(solution)/shard_map/nqkgd,nkde->nqkge/dot_general | solution.py:119
  257.3 0.5 fusion.70
  257.7 0.4 fusion.14
  258.1 0.8 fusion.8
  259.0 0.7 copy.28
  259.7 1.3 convert_element_type.138
  (18 shorter events, 0.2 us)
Async XLA Ops:
  6.5 2.2 copy-start.1
  6.5 92.0 %all-gather.7.cloned.1.call-start = ((), (), s32[]{:S(2)}) async-start(), calls=%async_computation | async-start | bytes 10485760 | tf_op jit(solution)/shard_map/all_gather | solution.py:71
  7.3 134.0 %all-gather.9.cloned.1.call-start = ((), (), s32[]{:S(2)}) async-start(), calls=%async_computation.1 | async-start | bytes 2228224 | tf_op jit(solution)/shard_map/all_gather | solution.py:81
  8.0 228.9 %all-gather.11.cloned.1.call-start = ((), (), s32[]{:S(2)}) async-start(), calls=%async_computation.2 | async-start | bytes 17825792 | tf_op jit(solution)/shard_map/all_gather | solution.py:76
  8.8 4.3 %collective-permute-start = (bf16[1,512,128]{2,1,0:T(8,128)(2,1)S(1)}, bf16[1,512,128]{2,1,0:T(8,128)(2,1)S(1)}, u32[]{:S(2)}, u32[]{:S(2)}) collective-permute-start(bf16[1,512,128]{2,1,0:T(8,128)(2,1)S(1)} %bitcast.143), channel_id=1, source_target_pairs={{0,16},{16,0},{32,48},{48,32},{64,80},{80,64},{96,112},{112,96},{1... | collective-permute-start | bytes 393224 | tf_op jit(solution)/shard_map/ppermute | solution.py:22
  13.1 7.6 %collective-permute-start.1 = (bf16[2,512,128]{2,1,0:T(8,128)(2,1)S(1)}, bf16[2,512,128]{2,1,0:T(8,128)(2,1)S(1)}, u32[]{:S(2)}, u32[]{:S(2)}) collective-permute-start(bf16[2,512,128]{2,1,0:T(8,128)(2,1)S(1)} %get-tuple-element.153), channel_id=1, source_target_pairs={{0,32},{16,48},{32,0},{48,16},{64,96},{80,112},{96,64},{112,80},{1... | collective-permute-start | bytes 786440 | tf_op jit(solution)/shard_map/ppermute | solution.py:22
  20.9 25.9 %collective-permute-start.2 = (bf16[4,512,128]{2,1,0:T(8,128)(2,1)S(1)}, bf16[4,512,128]{2,1,0:T(8,128)(2,1)S(1)}, u32[]{:S(2)}, u32[]{:S(2)}) collective-permute-start(bf16[4,512,128]{2,1,0:T(8,128)(2,1)S(1)} %bitcast.131), channel_id=1, source_target_pairs={{0,64},{16,80},{32,96},{48,112},{64,0},{80,16},{96,32},{112,48},{1... | collective-permute-start | bytes 1572872 | tf_op jit(solution)/shard_map/ppermute | solution.py:22
  46.8 5.5 %copy-start.2 = (f32[8]{0:T(128)S(1)}, f32[8]{0:T(128)}, u32[]{:S(2)}) copy-start(f32[8]{0:T(128)} %param.11) | copy-start | bytes 100
  47.1 50.6 %collective-permute-start.3 = (bf16[8,512,128]{2,1,0:T(8,128)(2,1)S(1)}, bf16[8,512,128]{2,1,0:T(8,128)(2,1)S(1)}, u32[]{:S(2)}, u32[]{:S(2)}) collective-permute-start(bf16[8,512,128]{2,1,0:T(8,128)(2,1)S(1)} %bitcast.129), channel_id=1, source_target_pairs={{0,128},{16,144},{32,160},{48,176},{64,192},{80,208},{96,224},{112... | collective-permute-start | bytes 3145736 | tf_op jit(solution)/shard_map/ppermute | solution.py:22
  148.2 103.4 %copy-start = (f32[4,1,128,128]{3,2,0,1:T(8,128)}, f32[4,1,128,128]{3,2,0,1:T(8,128)S(1)}, u32[]{:S(2)}) copy-start(f32[4,1,128,128]{3,2,0,1:T(8,128)S(1)} %fusion.47) | copy-start | bytes 786436
  251.9 2.5 slice-start
Sparse Core Ops, SparseCore 0:
  9.1 89.2 all-gather.6
  100.3 40.9 all-gather.8
  143.1 93.7 all-gather.10
